TPU v7x, 768 devices: a whole 4x8x12 slice. The times are simulated.
768 devices in a mesh: gx: 16 (over z_hi, y), gy: 48 (over z_lo, x, core).
Axes of the slice: x: 4, y: 8, z: 12 (z_hi: 2, z_lo: 6; z = z_hi * 6 + z_lo), core: 2. Of those that a mesh axis runs over, the one named last changes fastest.
Arguments:
- params: bfloat16 [768, 32, 192, 128], P(None, 'gx', 'gy'), may hold values from -6 to 6
- predicted: float32 [16, 48, 768, 128], P('gx', 'gy'), may hold values from -6 to 6
- measured_value: float32 [16, 48, 128], P('gx', 'gy'), may hold values from -6 to 6
- measurement_variance: float32 [16, 48, 128], P('gx', 'gy'), may hold values from 0.25 to 1
- observation_jitter: float32 [16, 48, 768, 128], P('gx', 'gy'), may hold values from -6 to 6
- obs_block: int32 [16, 48, 128], replicated, may hold values from 0 to 7
- taper_radius: int32 [32, 192], P('gx', 'gy'), may hold values from 1 to 2
- taper_pattern: int32 [32, 192, 25], P('gx', 'gy'), may hold values 0 or 1
Outputs:
- updated: bfloat16 [768, 32, 192, 128], P('gy', 'gx')
All inputs are finite; a program needn't handle non-finite values. No bound on the sum of `taper_pattern` on one device may be relied on, other than what follows from the above.
Results may differ from a plain program's by a relative error of at most 0.0039.
Values may be sent and summed in bfloat16 or wider, within the bound.
A program may use at most 32 MiB of HBM per device.

v0:
```python
import jax
import jax.numpy as jnp
from jax import lax
from jax.sharding import PartitionSpec as P

CELLS = 128
BLK_X = 2
BLK_Y = 4
OBS_TILE = 128
PATTERN = 25


def with_halo(cells, sides, width):
    for axis, dim in sides:
        count = lax.axis_size(axis)
        ends = count - 1
        head = lax.slice_in_dim(cells, 0, width, axis=dim)
        tail = lax.slice_in_dim(cells, cells.shape[dim] - width, cells.shape[dim], axis=dim)
        cells = jnp.concatenate(
            [
                lax.ppermute(tail, axis, [(i, (i + 1) % count) for i in range(ends)]),
                cells,
                lax.ppermute(head, axis, [((i + 1) % count, i) for i in range(ends)]),
            ],
            axis=dim,
        )
    return cells


def tapers(radius, pattern, own_x, own_y, obs_x, obs_y):
    step_x = obs_x[None, :] - own_x[:, None]
    step_y = obs_y[None, :] - own_y[:, None]
    inside = (jnp.abs(step_x) <= 2) & (jnp.abs(step_y) <= 2)
    offset = (step_x + 2) * 5 + (step_y + 2)
    slots = jnp.arange(PATTERN, dtype=jnp.int32)
    picked = jnp.sum(jnp.where(offset[:, :, None] == slots, pattern[:, None, :], 0), axis=2)
    reach = (radius + 1).astype(jnp.float32)
    spread = (step_x * step_x + step_y * step_y).astype(jnp.float32)
    shaped = jnp.maximum(1.0 - spread / (reach * reach)[:, None], 0.0)
    return jnp.where(inside, picked.astype(jnp.float32), 0.0) * shaped


def obs_places(obs_map, tiles_x, tiles_y):
    place_x = tiles_x[:, None, None] * BLK_X + obs_map // BLK_Y
    place_y = tiles_y[None, :, None] * BLK_Y + obs_map % BLK_Y
    return (place_x.reshape(-1), place_y.reshape(-1))


def contribution(anomaly, d_set, z_set, obs_map, tiles_x, tiles_y, own_x, own_y, radius, pattern):
    members = anomaly.shape[0]
    blocks = own_x.shape[0]
    place_x, place_y = obs_places(obs_map, tiles_x, tiles_y)
    weights = tapers(radius, pattern, own_x, own_y, place_x, place_y) / (members - 1)
    cross = lax.dot_general(
        anomaly, d_set, (((0,), (2,)), ((), ())), preferred_element_type=jnp.float32
    )
    complete_extent = cross.shape
    gain = (
        (cross.reshape(blocks, -1, weights.shape[1]) * weights[:, None, :])
        .reshape(complete_extent)
        .astype(jnp.bfloat16)
    )
    return lax.dot_general(
        z_set, gain, (((0, 1, 3), (1, 2, 3)), ((), ())), preferred_element_type=jnp.float32
    )


def weigh(d_tile, observation_residual, variance, obs_map):
    members = d_tile.shape[0]
    gram = jnp.dot(d_tile.T, d_tile, preferred_element_type=jnp.float32) / (members - 1)
    same = obs_map[:, None] == obs_map[None, :]
    system = jnp.where(same, gram, 0.0) + jnp.diag(variance)
    factor = jnp.linalg.cholesky(system)
    solved = jax.scipy.linalg.cho_solve((factor, True), observation_residual.T)
    return solved.T.astype(jnp.bfloat16)


def per_device(
    params,
    predicted,
    measured_value,
    measurement_variance,
    observation_jitter,
    obs_block,
    taper_radius,
    taper_pattern,
):
    members = params.shape[0]
    blocks = BLK_X * BLK_Y
    tile_x = lax.axis_index("gx")
    tile_y = lax.axis_index("gy")
    block_mean = jnp.mean(params.astype(jnp.float32), axis=0, keepdims=True)
    anomaly = (
        (params.astype(jnp.float32) - block_mean)
        .astype(jnp.bfloat16)
        .reshape(members, blocks * CELLS)
    )
    prior_state = predicted[0, 0]
    predicted_deviation = (prior_state - jnp.mean(prior_state, axis=0, keepdims=True)).astype(
        jnp.bfloat16
    )
    observation_residual = (
        measured_value[0, 0][None, :]
        + jnp.sqrt(measurement_variance[0, 0])[None, :] * observation_jitter[0, 0]
        - prior_state
    )
    map_pad = jnp.pad(obs_block, ((1, 1), (1, 1), (0, 0)))
    near_map = lax.dynamic_slice(map_pad, (tile_x, tile_y, jnp.int32(0)), (3, 3, OBS_TILE))
    weighted = weigh(
        predicted_deviation, observation_residual, measurement_variance[0, 0], near_map[1, 1]
    )
    stacked = jnp.stack([predicted_deviation, weighted])[None, None]
    radius = taper_radius.reshape(blocks)
    pattern = taper_pattern.reshape(blocks, PATTERN)
    local_ids = jnp.arange(blocks, dtype=jnp.int32)
    own_x = tile_x * BLK_X + local_ids // BLK_Y
    own_y = tile_y * BLK_Y + local_ids % BLK_Y
    adjacent_everything = jnp.arange(3, dtype=jnp.int32) - 1
    centre_x = tile_x + adjacent_everything
    centre_y = tile_y + adjacent_everything
    near = with_halo(stacked, (("gx", 0), ("gy", 1)), 1)
    delta = contribution(
        anomaly,
        near[:, :, 0],
        near[:, :, 1],
        near_map,
        centre_x,
        centre_y,
        own_x,
        own_y,
        radius,
        pattern,
    )
    updated = (params.astype(jnp.float32) + delta.reshape(members, BLK_X, BLK_Y, CELLS)).astype(
        jnp.bfloat16
    )
    return lax.all_to_all(updated, "gy", split_axis=0, concat_axis=2, tiled=True)


def solution(mesh):
    placed = (
        P(None, "gx", "gy", None),
        P("gx", "gy", None, None),
        P("gx", "gy", None),
        P("gx", "gy", None),
        P("gx", "gy", None, None),
        P(),
        P("gx", "gy"),
        P("gx", "gy", None),
    )
    return jax.shard_map(
        per_device, mesh=mesh, in_specs=placed, out_specs=P("gy", "gx", None, None), check_vma=False
    )
```

profile of v0, /device:TPU:57, one launch (start us, length us, event | category | flops | bytes accessed | tf_op | source)
XLA Modules:
  0.0 179.1 jit_solution(353071892744462002)
XLA Ops:
  0.0 0.7 bitcast_sqrt_fusion
  0.8 1.2 copy.42
  1.9 1.1 reduce_sum.27
  3.1 0.7 fusion.38
  4.5 11.7 %cholesky.16 = f32[128,128]{1,0:T(8,128)S(1)} custom-call(f32[128,128]{1,0:T(8,128)S(1)} %fusion.20), custom_call_target="Cholesky" | custom-call | tf_op jit(solution)/shard_map/jit(cholesky)/cholesky | solution.py:73
  17.5 9.8 %custom-call.10 = f32[1,128,128]{1,2,0:T(8,128)S(1)} custom-call(f32[1,128,128]{2,1,0:T(8,128)S(1)} %fusion.15), custom_call_target="InvertDiagBlocksLowerTriangular" | custom-call | tf_op jit(solution)/shard_map/jit(_cho_solve)/triangular_solve | solution.py:74
  28.6 3.0 %collective-permute-start.1 = (bf16[1,1,2,768,128]{3,4,2,1,0:T(8,128)(2,1)S(1)}, bf16[1,1,2,768,128]{3,4,2,1,0:T(8,128)(2,1)S(1)}, u32[]{:S(2)}, u32[]{:S(2)}) collective-permute-start(bf16[1,1,2,768,128]{3,4,2,1,0:T(8,128)(2,1)S(1)} %maximum_bitcast_fusion), channel_id=1, source_target_pairs={{48,0},{96,48},{144,96},{192,144},{240,192},{288,240},{336,288},{3... | collective-permute-start | bytes 1179656 | tf_op jit(solution)/shard_map/ppermute | solution.py:23
  31.6 13.0 %collective-permute-start = (bf16[1,1,2,768,128]{3,4,2,1,0:T(8,128)(2,1)S(1)}, bf16[1,1,2,768,128]{3,4,2,1,0:T(8,128)(2,1)S(1)}, u32[]{:S(2)}, u32[]{:S(2)}) collective-permute-start(bf16[1,1,2,768,128]{3,4,2,1,0:T(8,128)(2,1)S(1)} %maximum_bitcast_fusion), channel_id=1, source_target_pairs={{0,48},{48,96},{96,144},{144,192},{192,240},{240,288},{288,336},{3... | collective-permute-start | bytes 1179656 | tf_op jit(solution)/shard_map/ppermute | solution.py:21
  45.2 6.2 %collective-permute-done.1 = bf16[1,1,2,768,128]{3,4,2,1,0:T(8,128)(2,1)S(1)} collective-permute-done((bf16[1,1,2,768,128]{3,4,2,1,0:T(8,128)(2,1)S(1)}, bf16[1,1,2,768,128]{3,4,2,1,0:T(8,128)(2,1)S(1)}, u32[]{:S(2)}, u32[]{:S(2)}) %collective-permute-start.1) | collective-permute-done | bytes 393248 | tf_op jit(solution)/shard_map/ppermute | solution.py:23
  51.5 0.9 collective-permute-done
  52.3 1.2 pad_maximum_fusion.1
  53.5 3.4 %collective-permute-start.3 = (bf16[3,1,2,768,128]{3,4,2,1,0:T(8,128)(2,1)}, bf16[3,1,2,768,128]{3,4,2,1,0:T(8,128)(2,1)S(1)}, u32[]{:S(2)}, u32[]{:S(2)}) collective-permute-start(bf16[3,1,2,768,128]{3,4,2,1,0:T(8,128)(2,1)} %pad_maximum_fusion.1), channel_id=1, source_target_pairs={{1,0},{2,1},{3,2},{4,3},{5,4},{6,5},{7,6},{8,7},{9,8},{10,9},{11,1... | collective-permute-start | bytes 3538952 | tf_op jit(solution)/shard_map/ppermute | solution.py:23
  57.0 3.2 %collective-permute-start.2 = (bf16[3,1,2,768,128]{3,4,2,1,0:T(8,128)(2,1)}, bf16[3,1,2,768,128]{3,4,2,1,0:T(8,128)(2,1)}, u32[]{:S(2)}, u32[]{:S(2)}) collective-permute-start(bf16[3,1,2,768,128]{3,4,2,1,0:T(8,128)(2,1)} %pad_maximum_fusion.1), channel_id=1, source_target_pairs={{0,1},{1,2},{2,3},{3,4},{4,5},{5,6},{6,7},{7,8},{8,9},{9,10},{10,1... | collective-permute-start | bytes 3538952 | tf_op jit(solution)/shard_map/ppermute | solution.py:21
  60.4 1.6 copy.47
  62.3 9.8 %collective-permute-done.3 = bf16[3,1,2,768,128]{3,4,2,1,0:T(8,128)(2,1)S(1)} collective-permute-done((bf16[3,1,2,768,128]{3,4,2,1,0:T(8,128)(2,1)}, bf16[3,1,2,768,128]{3,4,2,1,0:T(8,128)(2,1)S(1)}, u32[]{:S(2)}, u32[]{:S(2)}) %collective-permute-start.3) | collective-permute-done | bytes 1179680 | tf_op jit(solution)/shard_map/ppermute | solution.py:23
  72.1 1.0 copy-done.7
  73.4 2.2 %pad_maximum_fusion = bf16[3,3,2,768,128]{3,4,2,1,0:T(8,128)(2,1)S(1)} fusion(bf16[3,1,2,768,128]{3,4,2,1,0:T(8,128)(2,1)} %copy-done.7, bf16[1,1,2,768,128]{3,4,2,1,0:T(8,128)(2,1)} %copy-done.3, bf16[1,1,2,768,128]{3,4,2,1,0:T(8,128)(2,1)} %copy-done.2, bf16[1,1,2,768,128]{3,4,2,1,0:T(8,128)(2,1)} %copy-done.4, ...), kind=kLoop, calls=%fused_computation.5 | loop fusion | flops 7077888 | bytes 7077888 | tf_op jit(solution)/shard_map/concatenate | solution.py:19
  75.8 1.3 copy-done.5
  77.0 3.6 %fusion = bf16[8,128,1152]{2,1,0:T(8,128)(2,1)} fusion(bf16[8,128,768]{2,1,0:T(8,128)(2,1)S(1)} %bitcast.70, bf16[1152,768,1]{1,0,2:T(8,128)(2,1)S(1)} %bitcast.69, f32[8,1152]{1,0:T(8,128)S(1)} %fusion.30), kind=kOutput, calls=%fused_computation.4 | convolution fusion | flops 1814298624 | bytes 5738496 | tf_op jit(solution)/shard_map/dot_general | solution.py:54
  80.7 4.3 %copy.49 = bf16[8,128,1152]{1,2,0:T(8,128)(2,1)} copy(bf16[8,128,1152]{2,1,0:T(8,128)(2,1)} %fusion) | data formatting | bytes 4718592 | tf_op jit(solution)/shard_map/convert_element_type | solution.py:61
  85.0 4.3 %fusion.2 = bf16[768,2,4,128]{3,0,2,1:T(8,128)(2,1)S(1)} fusion(bf16[2,4,128,3,3,128]{2,5,4,3,1,0:T(8,128)(2,1)} %bitcast.68, bf16[3,3,2,768,128]{3,4,2,1,0:T(8,128)(2,1)S(1)} %pad_maximum_fusion, bf16[768,2,4,128]{3,2,1,0:T(4,128)(2,1)} %param.8), kind=kOutput, calls=%fused_computation.7 | convolution fusion | flops 1814298624 | bytes 7274496 | tf_op jit(solution)/shard_map/dot_general | solution.py:63
  89.3 1.2 copy.52
  90.6 86.6 %all_to_all.18 = bf16[768,2,4,128]{3,2,1,0:T(4,128)(2,1)S(1)} all-to-all(bf16[768,2,4,128]{3,2,1,0:T(4,128)(2,1)S(1)} %copy.52), channel_id=1, replica_groups=mesh['gx'=16,'gy'=48] {'gy'}, dimensions={0} | all-to-all | bytes 3145728 | tf_op jit(solution)/shard_map/all_to_all | solution.py:137
  177.1 2.0 %copy.53 = bf16[16,2,48,4,128]{4,3,2,1,0:T(4,128)(2,1)} copy(bf16[16,2,48,4,128]{4,3,1,0,2:T(4,128)(2,1)S(1)} %bitcast.67) | data formatting | bytes 3145728 | tf_op jit(solution)/shard_map/all_to_all | solution.py:137
  (55 shorter events, 4.7 us)
Async XLA Ops:
  0.0 4.4 %copy-start.10 = (f32[1,1,128]{2,1,0:T(1,128)S(1)}, f32[1,1,128]{2,1,0:T(1,128)}, u32[]{:S(2)}) copy-start(f32[1,1,128]{2,1,0:T(1,128)} %param.11) | copy-start | bytes 1540
  0.0 4.0 %copy-start.1 = (f32[1,1,768,128]{3,2,1,0:T(8,128)S(1)}, f32[1,1,768,128]{3,2,1,0:T(8,128)}, u32[]{:S(2)}) copy-start(f32[1,1,768,128]{3,2,1,0:T(8,128)} %param.9) | copy-start | bytes 1179652
  0.0 27.3 %copy-start.8 = (f32[1,1,768,128]{3,2,1,0:T(8,128)S(1)}, f32[1,1,768,128]{3,2,1,0:T(8,128)}, u32[]{:S(2)}) copy-start(f32[1,1,768,128]{3,2,1,0:T(8,128)} %param.12) | copy-start | bytes 1179652
  0.0 27.3 %copy-start.12 = (f32[1,1,128]{2,1,0:T(1,128)S(1)}, f32[1,1,128]{2,1,0:T(1,128)}, u32[]{:S(2)}) copy-start(f32[1,1,128]{2,1,0:T(1,128)} %param.10) | copy-start | bytes 1540
  4.5 40.1 %copy-start = (bf16[768,2,4,128]{3,2,1,0:T(4,128)(2,1)S(1)}, bf16[768,2,4,128]{3,2,1,0:T(4,128)(2,1)}, u32[]{:S(2)}) copy-start(bf16[768,2,4,128]{3,2,1,0:T(4,128)(2,1)} %param.8) | copy-start | bytes 4718596
  27.9 16.8 %copy-start.6 = (s32[16,48,128]{2,1,0:T(8,128)S(1)}, s32[16,48,128]{2,1,0:T(8,128)}, u32[]{:S(2)}) copy-start(s32[16,48,128]{2,1,0:T(8,128)} %param.13) | copy-start | bytes 1179652
  28.6 23.8 %copy-start.2 = (bf16[1,1,2,768,128]{3,4,2,1,0:T(8,128)(2,1)}, bf16[1,1,2,768,128]{3,4,2,1,0:T(8,128)(2,1)S(1)}, u32[]{:S(2)}) copy-start(bf16[1,1,2,768,128]{3,4,2,1,0:T(8,128)(2,1)S(1)} %maximum_bitcast_fusion) | copy-start | bytes 1179652
  28.6 22.9 %collective-permute-start.1 = (bf16[1,1,2,768,128]{3,4,2,1,0:T(8,128)(2,1)S(1)}, bf16[1,1,2,768,128]{3,4,2,1,0:T(8,128)(2,1)S(1)}, u32[]{:S(2)}, u32[]{:S(2)}) collective-permute-start(bf16[1,1,2,768,128]{3,4,2,1,0:T(8,128)(2,1)S(1)} %maximum_bitcast_fusion), channel_id=1, source_target_pairs={{48,0},{96,48},{144,96},{192,144},{240,192},{288,240},{336,288},{3... | collective-permute-start | bytes 1179656 | tf_op jit(solution)/shard_map/ppermute | solution.py:23
  31.6 20.8 %collective-permute-start = (bf16[1,1,2,768,128]{3,4,2,1,0:T(8,128)(2,1)S(1)}, bf16[1,1,2,768,128]{3,4,2,1,0:T(8,128)(2,1)S(1)}, u32[]{:S(2)}, u32[]{:S(2)}) collective-permute-start(bf16[1,1,2,768,128]{3,4,2,1,0:T(8,128)(2,1)S(1)} %maximum_bitcast_fusion), channel_id=1, source_target_pairs={{0,48},{48,96},{96,144},{144,192},{192,240},{240,288},{288,336},{3... | collective-permute-start | bytes 1179656 | tf_op jit(solution)/shard_map/ppermute | solution.py:21
  45.2 15.0 %copy-start.11 = (s32[2,4]{1,0:T(2,128)S(1)}, s32[2,4]{1,0:T(2,128)}, u32[]{:S(2)}) copy-start(s32[2,4]{1,0:T(2,128)} %param.14) | copy-start | bytes 100
  45.2 15.1 %copy-start.9 = (s32[2,4,25]{2,1,0:T(4,128)S(1)}, s32[2,4,25]{2,1,0:T(4,128)}, u32[]{:S(2)}) copy-start(s32[2,4,25]{2,1,0:T(4,128)} %param.15) | copy-start | bytes 2404
  51.5 2.0 %copy-start.3 = (bf16[1,1,2,768,128]{3,4,2,1,0:T(8,128)(2,1)}, bf16[1,1,2,768,128]{3,4,2,1,0:T(8,128)(2,1)S(1)}, u32[]{:S(2)}) copy-start(bf16[1,1,2,768,128]{3,4,2,1,0:T(8,128)(2,1)S(1)} %collective-permute-done.1) | copy-start | bytes 1179652
  52.3 4.6 %copy-start.4 = (bf16[1,1,2,768,128]{3,4,2,1,0:T(8,128)(2,1)}, bf16[1,1,2,768,128]{3,4,2,1,0:T(8,128)(2,1)S(1)}, u32[]{:S(2)}) copy-start(bf16[1,1,2,768,128]{3,4,2,1,0:T(8,128)(2,1)S(1)} %collective-permute-done) | copy-start | bytes 1179652
  53.5 18.6 %collective-permute-start.3 = (bf16[3,1,2,768,128]{3,4,2,1,0:T(8,128)(2,1)}, bf16[3,1,2,768,128]{3,4,2,1,0:T(8,128)(2,1)S(1)}, u32[]{:S(2)}, u32[]{:S(2)}) collective-permute-start(bf16[3,1,2,768,128]{3,4,2,1,0:T(8,128)(2,1)} %pad_maximum_fusion.1), channel_id=1, source_target_pairs={{1,0},{2,1},{3,2},{4,3},{5,4},{6,5},{7,6},{8,7},{9,8},{10,9},{11,1... | collective-permute-start | bytes 3538952 | tf_op jit(solution)/shard_map/ppermute | solution.py:23
  57.0 16.5 %collective-permute-start.2 = (bf16[3,1,2,768,128]{3,4,2,1,0:T(8,128)(2,1)}, bf16[3,1,2,768,128]{3,4,2,1,0:T(8,128)(2,1)}, u32[]{:S(2)}, u32[]{:S(2)}) collective-permute-start(bf16[3,1,2,768,128]{3,4,2,1,0:T(8,128)(2,1)} %pad_maximum_fusion.1), channel_id=1, source_target_pairs={{0,1},{1,2},{2,3},{3,4},{4,5},{5,6},{6,7},{7,8},{8,9},{9,10},{10,1... | collective-permute-start | bytes 3538952 | tf_op jit(solution)/shard_map/ppermute | solution.py:21
  72.1 1.0 copy-start.7
  75.6 1.4 copy-start.5
where the time goes:
time: 180 us; the launch traced here: 179 us
  blocking collectives  86.6 us (48%)
  other arithmetic  28.6 us (16%)
  starting transfers between devices  22.6 us (13%)
  waiting for transfers between devices  17.2 us (10%)
  local copies, waits for them, and re-layouts  14.5 us (8%)
  matrix products  9.29 us (5%)
    all_to_all x1, blocking collectives, per_device(): lax.all_to_all(updated, 'gy', split_axis=0, concat_axis=2, tiled=True)  86.6 us
    ppermute x2, starting transfers between devices, with_halo(): lax.ppermute(tail, axis, [(i, (i + 1) % count) for i in range(ends)])  16.2 us
    ppermute x2, waiting for transfers between devices, with_halo(): lax.ppermute(head, axis, [((i + 1) % count, i) for i in range(ends)])  16.1 us
    another operation x3, other arithmetic, weigh(): factor = jnp.linalg.cholesky(system)  12.4 us
    another operation x2, other arithmetic, weigh(): solved = jax.scipy.linalg.cho_solve((factor, True), observation_residual.T)  10.5 us
    ppermute x2, starting transfers between devices, with_halo(): lax.ppermute(head, axis, [((i + 1) % count, i) for i in range(ends)])  6.42 us
    dot_general x1, matrix products, contribution(): lax.dot_general(z_set, gain, (((0, 1, 3), (1, 2, 3)), ((), ())), preferre...  4.35 us
    convert_element_type x1, local copies, waits for them, and re-layouts, contribution(): gain = (cross.reshape(blocks, -1, weights.shape[1]) * weights[:, None, :]...  4.3 us
  transfers between devices with their start and end apart: 4, of which 4 were waited for; matrix products, arithmetic and copies ran while one was open for 1% of the time, Pallas kernels for 0%

commit v1 on v0

v1 whole, which is shorter than its diff:
```python
import functools

import jax
import jax.numpy as jnp
from jax import lax
from jax.experimental import pallas as pl
from jax.experimental.pallas import tpu as pltpu
from jax.sharding import PartitionSpec as P

CELLS = 128
BLK_X = 2
BLK_Y = 4
OBS = 128
PATTERN = 25
BLOCKS = BLK_X * BLK_Y
TILES = 9
CENTRE = 4
NEWTON = 9
MESH = pl.DeviceIdType.MESH
EXACT = lax.Precision.HIGHEST


def taper_table(near_map, radius, pattern):
    tile = jnp.arange(TILES, dtype=jnp.int32)
    obs_x = ((tile // 3 - 1) * BLK_X)[:, None] + near_map // BLK_Y
    obs_y = ((tile % 3 - 1) * BLK_Y)[:, None] + near_map % BLK_Y
    own = jnp.arange(BLOCKS, dtype=jnp.int32)
    step_x = obs_x.reshape(1, -1) - (own // BLK_Y)[:, None]
    step_y = obs_y.reshape(1, -1) - (own % BLK_Y)[:, None]
    inside = (jnp.abs(step_x) <= 2) & (jnp.abs(step_y) <= 2)
    offset = (step_x + 2) * 5 + (step_y + 2)
    slots = jnp.arange(PATTERN, dtype=jnp.int32)
    picked = jnp.sum(jnp.where(offset[:, :, None] == slots, pattern[:, None, :], 0), axis=2)
    reach = (radius + 1).astype(jnp.float32)
    spread = (step_x * step_x + step_y * step_y).astype(jnp.float32)
    shaped = jnp.maximum(1.0 - spread / (reach * reach)[:, None], 0.0)
    return jnp.where(inside, picked.astype(jnp.float32), 0.0) * shaped


def inverse(system, least):
    size = system.shape[0]
    most = jnp.max(jnp.sum(jnp.abs(system), axis=0, keepdims=True), axis=1, keepdims=True)
    scale = 2.0 / (most + least)
    spread = (most - least) / (most + least)
    eye = (
        lax.broadcasted_iota(jnp.int32, (size, size), 0)
        == lax.broadcasted_iota(jnp.int32, (size, size), 1)
    )
    inv = jnp.where(eye, 2.0 * scale, 0.0) - (scale * scale) * system
    for _ in range(NEWTON):
        square = spread * spread
        scale = 2.0 / (2.0 - square)
        spread = square / (2.0 - square)
        turned = jnp.dot(system, inv, precision=EXACT, preferred_element_type=jnp.float32)
        step = jnp.dot(inv, turned, precision=EXACT, preferred_element_type=jnp.float32)
        inv = (2.0 * scale) * inv - (scale * scale) * step
    return inv


def front_kernel(
    rows,
    cols,
    pred_ref,
    jitter_ref,
    value_ref,
    var_ref,
    map_row_ref,
    map_col_ref,
    taper_ref,
    params_ref,
    out_ref,
    d_ref,
    w_ref,
    gain_ref,
    anom_ref,
    send_sem,
    recv_sem,
):
    members = pred_ref.shape[0]
    gx = lax.axis_index("gx")
    gy = lax.axis_index("gy")
    has_up = gx > 0
    has_down = gx < rows - 1
    has_left = gy > 0
    has_right = gy < cols - 1
    barrier = pltpu.get_barrier_semaphore()

    def greet(there, dev):
        @pl.when(there)
        def _():
            pl.semaphore_signal(barrier, inc=1, device_id=dev, device_id_type=MESH)

    up, down, left, right = (gx - 1, gy), (gx + 1, gy), (gx, gy - 1), (gx, gy + 1)
    greet(has_up, up)
    greet(has_down, down)
    greet(has_left, left)
    greet(has_right, right)

    def moves(kind):
        first = [(0, CENTRE, 1, has_down, down), (1, CENTRE, 7, has_up, up)]
        own = [(2, CENTRE, 3, has_right, right), (3, CENTRE, 5, has_left, left)]
        passed = [
            (4, 1, 0, has_right, right),
            (5, 1, 2, has_left, left),
            (6, 7, 6, has_right, right),
            (7, 7, 8, has_left, left),
        ]
        return first, own, passed

    bufs = (d_ref, w_ref)

    def copy(kind, move):
        index, src, dst, _, dev = move
        return pltpu.make_async_remote_copy(
            src_ref=bufs[kind].at[src],
            dst_ref=bufs[kind].at[dst],
            send_sem=send_sem.at[kind, index],
            recv_sem=recv_sem.at[kind, dst],
            device_id=dev,
            device_id_type=MESH,
        )

    def start(kind, group):
        for move in group:

            @pl.when(move[3])
            def _(move=move):
                copy(kind, move).start()

    def wait_sent(kind):
        for group in moves(kind):
            for move in group:

                @pl.when(move[3])
                def _(move=move):
                    copy(kind, move).wait_send()

    arrives = {
        1: has_up,
        7: has_down,
        0: has_left,
        3: has_left,
        6: has_left,
        2: has_right,
        5: has_right,
        8: has_right,
    }

    def wait_arrived(kind, slots):
        for slot in slots:

            @pl.when(arrives[slot])
            def _(slot=slot):
                pltpu.make_async_copy(
                    bufs[kind].at[slot], bufs[kind].at[slot], recv_sem.at[kind, slot]
                ).wait()

    for slot, there in arrives.items():

        @pl.when(jnp.logical_not(there))
        def _(slot=slot):
            d_ref[slot] = jnp.zeros(d_ref.shape[1:], d_ref.dtype)
            w_ref[slot] = jnp.zeros(w_ref.shape[1:], w_ref.dtype)

    pred = pred_ref[...]
    deviation = pred - jnp.sum(pred, axis=0, keepdims=True) / members
    d_own = deviation.astype(jnp.bfloat16)
    d_turned = deviation.T.astype(jnp.bfloat16)
    d_ref[CENTRE] = d_turned
    near = (
        has_up.astype(jnp.int32)
        + has_down.astype(jnp.int32)
        + has_left.astype(jnp.int32)
        + has_right.astype(jnp.int32)
    )
    pl.semaphore_wait(barrier, near)
    first, own, passed = moves(0)
    start(0, first)
    start(0, own)

    gram = jnp.dot(d_turned, d_own, preferred_element_type=jnp.float32) / (members - 1)
    same = map_col_ref[...] == map_row_ref[...]
    eye = (
        lax.broadcasted_iota(jnp.int32, (OBS, OBS), 0)
        == lax.broadcasted_iota(jnp.int32, (OBS, OBS), 1)
    )
    variance = var_ref[...]
    system = jnp.where(same, gram, 0.0) + jnp.where(eye, variance, 0.0)
    inv = inverse(system, jnp.min(variance, axis=1, keepdims=True))
    residual = value_ref[...] + jnp.sqrt(variance) * jitter_ref[...] - pred_ref[...]
    w_ref[CENTRE] = jnp.dot(
        residual, inv, precision=EXACT, preferred_element_type=jnp.float32
    ).astype(jnp.bfloat16)
    start(1, first)
    start(1, own)
    wait_arrived(0, (1, 7))
    start(0, passed)

    for block in range(BLOCKS):
        cells = slice(block * CELLS, (block + 1) * CELLS)
        wide = params_ref[:, cells].astype(jnp.float32)
        mean = jnp.sum(wide, axis=0, keepdims=True) / members
        anom_ref[:, cells] = (wide - mean).astype(jnp.bfloat16)

    wait_arrived(1, (1, 7))
    start(1, passed)
    wait_arrived(0, (3, 5, 0, 2, 6, 8))

    def gain_of(tile):
        cross = jnp.dot(d_ref[tile], anom_ref[...], preferred_element_type=jnp.float32)
        rows_of = pl.ds(pl.multiple_of(tile * OBS, OBS), OBS)
        weight = taper_ref[rows_of, :]
        for block in range(BLOCKS):
            cells = slice(block * CELLS, (block + 1) * CELLS)
            gain_ref[rows_of, cells] = (cross[:, cells] * weight[:, block : block + 1]).astype(
                jnp.bfloat16
            )

    @pl.loop(0, TILES)
    def _(tile):
        gain_of(tile)

    wait_arrived(1, (3, 5, 0, 2, 6, 8))
    part = 256

    @pl.loop(0, members // part)
    def _(step):
        who = pl.ds(pl.multiple_of(step * part, part), part)
        lhs = jnp.concatenate([w_ref[tile, who, :] for tile in range(TILES)], axis=1)
        for chunk in range(BLOCKS // 2):
            cells = slice(chunk * 256, (chunk + 1) * 256)
            delta = jnp.dot(lhs, gain_ref[:, cells], preferred_element_type=jnp.float32)
            out_ref[who, cells] = (params_ref[who, cells].astype(jnp.float32) + delta).astype(
                jnp.bfloat16
            )

    wait_sent(0)
    wait_sent(1)


def front(rows, cols, pred, jitter, value, var, map_row, map_col, taper, params):
    members = pred.shape[0]
    vmem = pl.BlockSpec(memory_space=pltpu.VMEM)
    return pl.pallas_call(
        functools.partial(front_kernel, rows, cols),
        out_shape=jax.ShapeDtypeStruct(params.shape, jnp.bfloat16),
        in_specs=[vmem] * 8,
        out_specs=vmem,
        scratch_shapes=[
            pltpu.VMEM((TILES, OBS, members), jnp.bfloat16),
            pltpu.VMEM((TILES, members, OBS), jnp.bfloat16),
            pltpu.VMEM((TILES * OBS, BLOCKS * CELLS), jnp.bfloat16),
            pltpu.VMEM((members, BLOCKS * CELLS), jnp.bfloat16),
            pltpu.SemaphoreType.DMA((2, 8)),
            pltpu.SemaphoreType.DMA((2, TILES)),
        ],
        compiler_params=pltpu.CompilerParams(
            collective_id=0, has_side_effects=True, vmem_limit_bytes=40 << 20
        ),
    )(pred, jitter, value, var, map_row, map_col, taper, params)


def regroup_kernel(count, send_ref, recv_ref, own_sem, send_sem, recv_sem):
    gx = lax.axis_index("gx")
    me = lax.axis_index("gy")
    share = recv_ref.shape[1]
    barrier = pltpu.get_barrier_semaphore()

    def greet(step, carry):
        pl.semaphore_signal(
            barrier, inc=1, device_id=(gx, lax.rem(me + step, count)), device_id_type=MESH
        )
        return carry

    def rows_for(target):
        return send_ref.at[pl.ds(pl.multiple_of(target * share, share), share), :]

    lax.fori_loop(1, count, greet, 0)
    own = pltpu.make_async_copy(rows_for(me), recv_ref.at[me], own_sem)
    own.start()
    pl.semaphore_wait(barrier, count - 1)

    def send(step, carry):
        target = lax.rem(me + step, count)
        pltpu.make_async_remote_copy(
            src_ref=rows_for(target),
            dst_ref=recv_ref.at[me],
            send_sem=send_sem,
            recv_sem=recv_sem,
            device_id=(gx, target),
            device_id_type=MESH,
        ).start()
        return carry

    lax.fori_loop(1, count, send, 0)
    others = recv_ref.at[pl.ds(0, count - 1)]
    pltpu.make_async_copy(others, others, send_sem).wait()
    pltpu.make_async_copy(others, others, recv_sem).wait()
    own.wait()


def regroup(count, updated):
    members, cells = updated.shape
    vmem = pl.BlockSpec(memory_space=pltpu.VMEM)
    return pl.pallas_call(
        functools.partial(regroup_kernel, count),
        out_shape=jax.ShapeDtypeStruct((count, members // count, cells), updated.dtype),
        in_specs=[vmem],
        out_specs=vmem,
        scratch_shapes=[pltpu.SemaphoreType.DMA] * 3,
        compiler_params=pltpu.CompilerParams(collective_id=1, has_side_effects=True),
    )(updated)


def per_device(
    rows,
    cols,
    params,
    predicted,
    measured_value,
    measurement_variance,
    observation_jitter,
    obs_block,
    taper_radius,
    taper_pattern,
):
    members = params.shape[0]
    tile_x = lax.axis_index("gx")
    tile_y = lax.axis_index("gy")
    map_pad = jnp.pad(obs_block, ((1, 1), (1, 1), (0, 0)))
    near_map = lax.dynamic_slice(map_pad, (tile_x, tile_y, jnp.int32(0)), (3, 3, OBS)).reshape(
        TILES, OBS
    )
    taper = taper_table(
        near_map, taper_radius.reshape(BLOCKS), taper_pattern.reshape(BLOCKS, PATTERN)
    ) / (members - 1)
    own_map = near_map[CENTRE]
    updated = front(
        rows,
        cols,
        predicted[0, 0],
        observation_jitter[0, 0],
        measured_value[0],
        measurement_variance[0],
        own_map[None, :],
        own_map[:, None],
        taper.T,
        params.reshape(members, BLOCKS * CELLS),
    )
    regrouped = regroup(cols, updated)
    share = members // cols
    out = regrouped.reshape(cols, share, BLK_X, BLK_Y, CELLS).transpose(1, 2, 0, 3, 4)
    return out.reshape(share, BLK_X, cols * BLK_Y, CELLS)


def solution(mesh):
    placed = (
        P(None, "gx", "gy", None),
        P("gx", "gy", None, None),
        P("gx", "gy", None),
        P("gx", "gy", None),
        P("gx", "gy", None, None),
        P(),
        P("gx", "gy"),
        P("gx", "gy", None),
    )
    body = functools.partial(per_device, mesh.shape["gx"], mesh.shape["gy"])
    return jax.shard_map(
        body, mesh=mesh, in_specs=placed, out_specs=P("gy", "gx", None, None), check_vma=False
    )
```

time: 180 us -> 130 us (0.72)
  the two profiles are of different devices: /device:TPU:57 before, /device:TPU:191 now
where the time goes in v1:
time: 130 us; the launch traced here: 129 us
  Pallas kernels  116 us (89%)
  local copies, waits for them, and re-layouts  10.9 us (8%)
  other arithmetic  1.75 us (1%)
    pallas_call x1, Pallas kernels, regroup(): pl.pallas_call(functools.partial(regroup_kernel, count), out_shape=jax.Sh...  70.8 us
    pallas_call x1, Pallas kernels, front(): pl.pallas_call(functools.partial(front_kernel, rows, cols), out_shape=jax...  45.6 us
    reshape x1, local copies, waits for them, and re-layouts, per_device(): params.reshape(members, BLOCKS * CELLS)  2.89 us
    reshape x1, local copies, waits for them, and re-layouts, per_device(): regrouped.reshape(cols, share, BLK_X, BLK_Y, CELLS).transpose(1, 2, 0, 3, 4)  2.83 us

profile of v1, /device:TPU:191, one launch (start us, length us, event | category | flops | bytes accessed | tf_op | source)
XLA Modules:
  0.0 129.2 jit_solution(10117198768267304108)
XLA Ops:
  0.0 0.7 convert_multiply_fusion
  0.7 0.1 mul.53
  0.8 0.8 pad_dynamic-slice_fusion
  1.6 0.1 fusion.10
  1.7 0.8 copy.16
  2.5 0.1 add_add_fusion
  2.5 0.2 select_reduce_fusion
  2.7 0.1 copy.18.map_col_ref
  2.8 0.2 copy.17
  3.1 0.7 fusion.7.taper_ref
  3.8 0.0 copy-start.1
  3.8 0.0 copy-start.2
  3.8 0.0 copy-start.3
  3.9 0.0 copy-start.4
  3.9 2.9 %reshape.197.params_ref = bf16[768,1024]{1,0:T(8,128)(2,1)S(1)} reshape(bf16[768,2,4,128]{3,2,1,0:T(4,128)(2,1)} %param.8) | data formatting | bytes 3145728 | tf_op jit(solution)/shard_map/reshape | solution.py:348
  6.8 0.0 copy-done.1
  6.8 0.0 copy-done.2
  6.8 0.0 copy-done.3
  6.8 45.6 %shard_map.82.send_ref = bf16[768,1024]{1,0:T(8,128)(2,1)S(1)} custom-call(f32[768,128]{1,0:T(8,128)S(1)} %bitcast.17, f32[768,128]{1,0:T(8,128)S(1)} %bitcast.18, f32[1,128]{1,0:T(1,128)S(1)} %bitcast.19, f32[1,128]{1,0:T(1,128)S(1)} %bitcast.20, s32[1,128]{1,0:T(1,128)S(1)} %get-tuple-element.8.map_row_ref, s32[128,1]{1,0:T(8,128)S(1)} %copy.18.map_col_ref, ...), custom_call_target="tpu_custom_call" | custom-call | tf_op jit(solution)/shard_map/pallas_call | solution.py:244
  52.4 0.0 copy-start
  52.4 1.1 copy-done
  53.6 70.8 %shard_map.83 = bf16[48,16,1024]{2,1,0:T(8,128)(2,1)} custom-call(bf16[768,1024]{1,0:T(8,128)(2,1)} %copy-done), custom_call_target="tpu_custom_call" | custom-call | tf_op jit(solution)/shard_map/pallas_call | solution.py:305
  124.4 2.8 %reshape.198 = bf16[48,16,2,4,128]{4,3,2,1,0:T(4,128)(2,1)S(1)} reshape(bf16[48,16,1024]{2,1,0:T(8,128)(2,1)} %shard_map.83) | data formatting | bytes 3145728 | tf_op jit(solution)/shard_map/reshape | solution.py:352
  127.2 2.0 %copy.19 = bf16[16,2,48,4,128]{4,3,2,1,0:T(4,128)(2,1)} copy(bf16[16,2,48,4,128]{4,3,1,0,2:T(4,128)(2,1)S(1)} %bitcast.21) | data formatting | bytes 3145728 | tf_op jit(solution)/shard_map/transpose | solution.py:352
  (7 shorter events, 0.0 us)
Async XLA Ops:
  3.8 2.9 %copy-start.1 = (f32[1,1,768,128]{3,2,1,0:T(8,128)S(1)}, f32[1,1,768,128]{3,2,1,0:T(8,128)}, u32[]{:S(2)}) copy-start(f32[1,1,768,128]{3,2,1,0:T(8,128)} %param.9) | copy-start | bytes 1179652
  3.8 2.9 %copy-start.2 = (f32[1,1,768,128]{3,2,1,0:T(8,128)S(1)}, f32[1,1,768,128]{3,2,1,0:T(8,128)}, u32[]{:S(2)}) copy-start(f32[1,1,768,128]{3,2,1,0:T(8,128)} %param.12) | copy-start | bytes 1179652
  3.8 2.9 %copy-start.3 = (f32[1,1,128]{2,1,0:T(1,128)S(1)}, f32[1,1,128]{2,1,0:T(1,128)}, u32[]{:S(2)}) copy-start(f32[1,1,128]{2,1,0:T(1,128)} %param.10) | copy-start | bytes 1540
  3.9 2.9 %copy-start.4 = (f32[1,1,128]{2,1,0:T(1,128)S(1)}, f32[1,1,128]{2,1,0:T(1,128)}, u32[]{:S(2)}) copy-start(f32[1,1,128]{2,1,0:T(1,128)} %param.11) | copy-start | bytes 1540
  52.4 1.1 copy-start

commit v2 on v0

v2 whole, which is shorter than its diff:
```python
import functools

import jax
import jax.numpy as jnp
from jax import lax
from jax.experimental import pallas as pl
from jax.experimental.pallas import tpu as pltpu
from jax.sharding import PartitionSpec as P

CELLS = 128
BLK_X = 2
BLK_Y = 4
OBS = 128
PATTERN = 25
BLOCKS = BLK_X * BLK_Y
TILES = 9
UP, CENTRE, DOWN = 3, 4, 5
NEWTON = 9
PIECES = 6
ROUNDS = 3
MESH = pl.DeviceIdType.MESH
EXACT = lax.Precision.HIGHEST


def mm(a, b, precision=None):
    return jnp.dot(a, b, precision=precision, preferred_element_type=jnp.float32)


def newton_start(system, least):
    size = system.shape[0]
    most = jnp.max(jnp.sum(jnp.abs(system), axis=0, keepdims=True), axis=1, keepdims=True)
    scale = 2.0 / (most + least)
    spread = (most - least) / (most + least)
    eye = (
        lax.broadcasted_iota(jnp.int32, (size, size), 0)
        == lax.broadcasted_iota(jnp.int32, (size, size), 1)
    )
    return jnp.where(eye, 2.0 * scale, 0.0) - (scale * scale) * system, spread


def newton(system, inv, spread, steps):
    for _ in range(steps):
        square = spread * spread
        scale = 2.0 / (2.0 - square)
        spread = square / (2.0 - square)
        step = mm(inv, mm(system, inv, EXACT), EXACT)
        inv = (2.0 * scale) * inv - (scale * scale) * step
    return inv, spread


def kernel(
    rows,
    cols,
    radius_ref,
    pred_ref,
    jitter_ref,
    value_ref,
    var_ref,
    map_ref,
    pattern_ref,
    params_hbm,
    recv_ref,
    params_ref,
    d_ref,
    w_ref,
    gain_ref,
    anom_ref,
    wide_ref,
    delta_ref,
    taper_ref,
    sent_ref,
    d_near,
    d_far,
    w_near,
    w_far,
    load_sem,
    own_sem,
    all_send,
    all_recv,
    d_send,
    d_recv,
    w_send,
    w_recv,
    d_relay,
    w_relay,
):
    members = pred_ref.shape[0]
    piece = members // PIECES
    half = rows // 2
    share = members // cols
    gx = lax.axis_index("gx")
    gy = lax.axis_index("gy")
    lower = gx < half
    upper = gx >= half
    low_seam = gx == half - 1
    high_seam = gx == half
    seam = (gx == half - 1) | (gx == half)
    relay = jnp.logical_not(seam)
    column = lax.rem(gx, half)
    across = lax.rem(gx + half, rows)
    has_left = gy > 0
    has_right = gy < cols - 1
    sends_up = (gx > 0) & jnp.logical_not(high_seam)
    sends_down = (gx < rows - 1) & jnp.logical_not(low_seam)

    params_load = pltpu.make_async_copy(params_hbm, params_ref, load_sem)
    params_load.start()

    barrier = pltpu.get_barrier_semaphore()

    def greet(dev):
        pl.semaphore_signal(barrier, inc=1, device_id=dev, device_id_type=MESH)

    def greet_group(step, carry):
        greet((gx, lax.rem(gy + step, cols)))
        return carry

    lax.fori_loop(1, cols, greet_group, 0)
    greet((across, gy))

    @pl.when(sends_up)
    def _():
        greet((gx - 1, gy))

    @pl.when(sends_down)
    def _():
        greet((gx + 1, gy))

    for side, is_side, is_seam, at in (
        (0, lower, low_seam, half - 1),
        (half, upper, high_seam, half),
    ):

        @pl.when(is_side & relay)
        def _(at=at):
            greet((at, gy))

        @pl.when(is_seam)
        def _(side=side, at=at):
            for target in range(side, side + half):
                if target != at:
                    greet((target, gy))

    greetings = (
        cols
        + sends_up.astype(jnp.int32)
        + sends_down.astype(jnp.int32)
        + 1
        + (half - 2) * seam.astype(jnp.int32)
    )

    def remote(src, dst, send, recv, dev):
        return pltpu.make_async_remote_copy(
            src_ref=src,
            dst_ref=dst,
            send_sem=send,
            recv_sem=recv,
            device_id=dev,
            device_id_type=MESH,
        )

    class Parcel:
        def __init__(self, buf, start, size, near, far, send, recv, relays):
            self.buf, self.start, self.size = buf, start, size
            self.near, self.far, self.send, self.recv, self.relays = near, far, send, recv, relays
            self.part = size // half

        def rows_of(self, slot):
            return self.buf.at[slot, pl.ds(self.start, self.size), :]

        def part_of(self, slot, index):
            offset = pl.multiple_of(self.start + index * self.part, self.part)
            return self.buf.at[slot, pl.ds(offset, self.part), :]

        def hop(self, index, src, dst, dev):
            return remote(
                self.rows_of(src), self.rows_of(dst), self.send.at[index], self.recv.at[dst], dev
            )

        def own_hops(self):
            return (
                (sends_down, self.hop(0, CENTRE, UP, (gx + 1, gy))),
                (sends_up, self.hop(1, CENTRE, DOWN, (gx - 1, gy))),
                (has_right, self.hop(2, CENTRE, 1, (gx, gy + 1))),
                (has_left, self.hop(3, CENTRE, 7, (gx, gy - 1))),
            )

        def passed_hops(self):
            return (
                (has_right, self.hop(4, UP, 0, (gx, gy + 1))),
                (has_left, self.hop(5, UP, 6, (gx, gy - 1))),
                (has_right, self.hop(6, DOWN, 2, (gx, gy + 1))),
                (has_left, self.hop(7, DOWN, 8, (gx, gy - 1))),
            )

        def seam_hops(self):
            hops = []
            for side, is_seam, at in ((0, low_seam, half - 1), (half, high_seam, half)):
                for index in range(half):
                    if side + index == at:
                        dst, recv, dev = self.far, self.relays.at[1], (across, gy)
                    else:
                        dst, recv, dev = self.near, self.relays.at[0], (side + index, gy)
                    src = self.part_of(CENTRE, index)
                    hops.append((is_seam, remote(src, dst, self.send.at[8 + index], recv, dev)))
            return hops

        def cross_hops(self):
            low_end, high_end = gx == 0, gx == rows - 1
            inner = relay & jnp.logical_not(low_end) & jnp.logical_not(high_end)
            send, dev = self.send.at[8], (across, gy)
            return (
                (inner, remote(self.near, self.far, send, self.relays.at[1], dev)),
                (low_end, remote(self.near, self.part_of(UP, 0), send, self.recv.at[UP], dev)),
                (
                    high_end,
                    remote(self.near, self.part_of(DOWN, half - 1), send, self.recv.at[DOWN], dev),
                ),
            )

        def last_hops(self):
            hops = []
            for is_side, at, slot in ((lower, half - 1, DOWN), (upper, half, UP)):
                dst = self.part_of(slot, column)
                hop = remote(self.far, dst, self.send.at[9], self.recv.at[slot], (at, gy))
                hops.append((is_side & relay, hop))
            return hops

        def wait_near(self):
            @pl.when(relay)
            def _():
                pltpu.make_async_copy(self.near, self.near, self.relays.at[0]).wait()

        def wait_far(self):
            @pl.when(relay)
            def _():
                pltpu.make_async_copy(self.far, self.far, self.relays.at[1]).wait()

        def wait_slots(self, slots, where=None):
            for slot in slots:
                there = arrives[slot] if where is None else arrives[slot] & where

                @pl.when(there)
                def _(slot=slot):
                    ref = self.rows_of(slot)
                    pltpu.make_async_copy(ref, ref, self.recv.at[slot]).wait()

        def start_own(self):
            start(self.own_hops())
            start(self.seam_hops())

        def cross(self):
            self.wait_near()
            start(self.cross_hops())

        def last(self):
            self.wait_far()
            start(self.last_hops())

        def pass_on(self, where):
            self.wait_slots((UP, DOWN), where)
            start(self.passed_hops(), where)

        def wait_sent(self):
            for hops in (
                self.own_hops(),
                self.passed_hops(),
                self.seam_hops(),
                self.cross_hops(),
                self.last_hops(),
            ):
                for there, hop in hops:

                    @pl.when(there)
                    def _(hop=hop):
                        hop.wait_send()

    def start(hops, where=None):
        for there, hop in hops:

            @pl.when(there if where is None else there & where)
            def _(hop=hop):
                hop.start()

    arrives = {UP: gx > 0, DOWN: gx < rows - 1}
    arrives.update({slot: has_left for slot in (0, 1, 2)})
    arrives.update({slot: has_right for slot in (6, 7, 8)})

    for slot, there in arrives.items():

        @pl.when(jnp.logical_not(there))
        def _(slot=slot):
            d_ref[slot] = jnp.zeros(d_ref.shape[1:], d_ref.dtype)
            w_ref[slot] = jnp.zeros(w_ref.shape[1:], w_ref.dtype)

    d_parcel = Parcel(d_ref, 0, OBS, d_near, d_far, d_send, d_recv, d_relay)
    w_parcels = [
        Parcel(
            w_ref,
            turn * 2 * piece,
            2 * piece,
            w_near.at[turn],
            w_far.at[turn],
            w_send.at[turn],
            w_recv.at[turn],
            w_relay.at[turn],
        )
        for turn in range(ROUNDS)
    ]

    pred = pred_ref[...]
    deviation = pred - jnp.sum(pred, axis=0, keepdims=True) / members
    d_own = deviation.astype(jnp.bfloat16)
    d_turned = deviation.T.astype(jnp.bfloat16)
    d_ref[CENTRE] = d_turned
    pl.semaphore_wait(barrier, greetings)
    d_parcel.start_own()

    gram = mm(d_turned, d_own) / (members - 1)
    own_map = jnp.broadcast_to(map_ref[gx, pl.ds(gy, 1), :].astype(jnp.float32), (OBS, OBS))
    eye = (
        lax.broadcasted_iota(jnp.int32, (OBS, OBS), 0)
        == lax.broadcasted_iota(jnp.int32, (OBS, OBS), 1)
    )
    variance = var_ref[...]
    system = jnp.where(own_map == own_map.T, gram, 0.0) + jnp.where(eye, variance, 0.0)
    inv, spread = newton_start(system, jnp.min(variance, axis=1, keepdims=True))
    inv, spread = newton(system, inv, spread, 4)
    d_parcel.cross()
    inv, spread = newton(system, inv, spread, NEWTON - 4)
    deviation_scale = jnp.sqrt(variance)
    for turn in range(ROUNDS):
        for place, which in enumerate((turn, PIECES - 1 - turn)):
            who = slice(which * piece, (which + 1) * piece)
            residual = (
                value_ref[...] + deviation_scale * jitter_ref[who, :] - pred_ref[who, :]
            )
            at = (2 * turn + place) * piece
            w_ref[CENTRE, at : at + piece, :] = mm(residual, inv, EXACT).astype(jnp.bfloat16)
        w_parcels[turn].start_own()

    d_parcel.pass_on(relay)
    d_parcel.last()

    block = lax.broadcasted_iota(jnp.int32, (BLOCKS, OBS), 0)
    reach = jnp.zeros((BLOCKS, OBS), jnp.int32)
    for index in range(BLOCKS):
        reach = jnp.where(block == index, radius_ref[index // BLK_Y, index % BLK_Y] + 1, reach)
    reach = reach.astype(jnp.float32)
    reach = reach * reach
    listed = [
        jnp.broadcast_to(pattern_ref[:, slot : slot + 1], (BLOCKS, OBS)) for slot in range(PATTERN)
    ]
    for tile in range(TILES):
        at_x = lax.rem(gx + rows + tile % 3 - 1, rows)
        at_y = lax.rem(gy + cols + tile // 3 - 1, cols)
        near = jnp.broadcast_to(map_ref[at_x, pl.ds(at_y, 1), :], (BLOCKS, OBS))
        step_x = (tile % 3 - 1) * BLK_X + (near >> 2) - (block >> 2)
        step_y = (tile // 3 - 1) * BLK_Y + (near & 3) - (block & 3)
        inside = (jnp.abs(step_x) <= 2) & (jnp.abs(step_y) <= 2)
        offset = (step_x + 2) * 5 + (step_y + 2)
        picked = jnp.zeros((BLOCKS, OBS), jnp.int32)
        for slot in range(PATTERN):
            picked = jnp.where(offset == slot, listed[slot], picked)
        distance = (step_x * step_x + step_y * step_y).astype(jnp.float32)
        shaped = jnp.maximum(1.0 - distance / reach, 0.0)
        taper = jnp.where(inside, picked.astype(jnp.float32), 0.0) * shaped / (members - 1)
        filled = jnp.concatenate([taper, jnp.zeros((OBS - BLOCKS, OBS), jnp.float32)], axis=0)
        taper_ref[tile * OBS : (tile + 1) * OBS, :] = filled.T

    params_load.wait()
    batch = 64

    def batch_rows(step):
        return pl.ds(pl.multiple_of(step * batch * BLOCKS, batch * BLOCKS), batch * BLOCKS)

    def batch_of(step):
        wide = params_ref[batch_rows(step), :].astype(jnp.float32)
        return wide.reshape(batch, BLOCKS, CELLS)

    mean = lax.fori_loop(
        0,
        members // batch,
        lambda step, total: total + jnp.sum(batch_of(step), axis=0),
        jnp.zeros((BLOCKS, CELLS), jnp.float32),
    ) * (1.0 / members)

    @pl.loop(0, members // batch)
    def _(step):
        centred = batch_of(step) - mean[None]
        wide_ref[batch_rows(step), :] = centred.reshape(batch * BLOCKS, CELLS)

    for index in range(BLOCKS):
        for first in range(0, members, 256):
            anom_ref[first : first + 256, index * CELLS : (index + 1) * CELLS] = wide_ref[
                pl.ds(first * BLOCKS + index, 256, stride=BLOCKS), :
            ].astype(jnp.bfloat16)

    near_tiles = 6
    obs = near_tiles * OBS

    def first_slot(group):
        return 3 * (group % 2)

    def gain_of(group):
        cells = slice(group * 2 * CELLS, (group + 1) * 2 * CELLS)
        first = first_slot(group)
        d_set = d_ref[first : first + near_tiles].reshape(obs, members)
        cross = mm(d_set, anom_ref[:, cells])
        weight = taper_ref[first * OBS : first * OBS + obs, :]
        for side in range(2):
            index = 2 * group + side
            gain_ref[group, :, side * CELLS : (side + 1) * CELLS] = (
                cross[:, side * CELLS : (side + 1) * CELLS] * weight[:, index : index + 1]
            ).astype(jnp.bfloat16)

    w_parcels[0].cross()
    w_parcels[0].pass_on(relay)
    w_parcels[1].cross()
    d_parcel.pass_on(seam)
    d_parcel.wait_slots((1, 7, 0, 2, 6, 8))
    gain_of(0)
    gain_of(1)
    w_parcels[0].last()
    w_parcels[1].pass_on(relay)
    w_parcels[2].cross()
    gain_of(2)
    gain_of(3)

    fan = cols // PIECES

    def send_rows(target):
        size = share * BLOCKS
        return sent_ref.at[pl.ds(pl.multiple_of(target * size, size), size), :]

    own_copy = pltpu.make_async_copy(send_rows(gy), recv_ref.at[gy], own_sem)
    far_side = lax.div(2 * gy, cols)

    def finish(turn):
        w_parcels[turn].pass_on(seam)
        w_parcels[turn].wait_slots((1, 7, 0, 2, 6, 8))
        who = slice(turn * 2 * piece, (turn + 1) * 2 * piece)
        for group in range(BLOCKS // 2):
            first = first_slot(group)
            w_set = jnp.concatenate(
                [w_ref[slot, who, :] for slot in range(first, first + near_tiles)], axis=1
            )
            delta = mm(w_set, gain_ref[group])
            for side in range(2):
                delta_ref[pl.ds(2 * group + side, 2 * piece, stride=BLOCKS), :] = delta[
                    :, side * CELLS : (side + 1) * CELLS
                ]
        size = piece * BLOCKS
        for place, which in enumerate((turn, PIECES - 1 - turn)):
            to = slice(which * size, (which + 1) * size)
            sent_ref[to, :] = (
                params_ref[to, :].astype(jnp.float32)
                + delta_ref[place * size : (place + 1) * size, :]
            ).astype(jnp.bfloat16)
        other, near = PIECES - 1 - turn, turn
        for which in (
            other + far_side * (near - other),
            near + far_side * (other - near),
        ):

            def send(step, carry, which=which):
                target = which * fan + lax.rem(step + gy, fan)

                @pl.when(target != gy)
                def _():
                    remote(
                        send_rows(target), recv_ref.at[gy], all_send, all_recv, (gx, target)
                    ).start()

                @pl.when(target == gy)
                def _():
                    own_copy.start()

                return carry

            lax.fori_loop(0, fan, send, 0)

    finish(0)
    w_parcels[1].last()
    w_parcels[2].pass_on(relay)
    finish(1)
    w_parcels[2].last()
    finish(2)

    others = recv_ref.at[pl.ds(0, cols - 1)]
    d_parcel.wait_sent()
    for parcel in w_parcels:
        parcel.wait_sent()
    own_copy.wait()
    pltpu.make_async_copy(others, others, all_send).wait()
    pltpu.make_async_copy(others, others, all_recv).wait()


def per_device(
    rows,
    cols,
    params,
    predicted,
    measured_value,
    measurement_variance,
    observation_jitter,
    obs_block,
    taper_radius,
    taper_pattern,
):
    members = params.shape[0]
    share = members // cols
    half = rows // 2
    cells = BLOCKS * CELLS
    turn = members // ROUNDS
    vmem = pl.BlockSpec(memory_space=pltpu.VMEM)
    smem = pl.BlockSpec(memory_space=pltpu.SMEM)
    anywhere = pl.BlockSpec(memory_space=pl.ANY)
    dma = pltpu.SemaphoreType.DMA
    bf16, f32 = jnp.bfloat16, jnp.float32
    regrouped = pl.pallas_call(
        functools.partial(kernel, rows, cols),
        out_shape=jax.ShapeDtypeStruct((cols, share * BLOCKS, CELLS), bf16),
        in_specs=[smem] + [vmem] * 6 + [anywhere],
        out_specs=anywhere,
        scratch_shapes=[
            pltpu.VMEM((members * BLOCKS, CELLS), bf16),
            pltpu.VMEM((TILES, OBS, members), bf16),
            pltpu.VMEM((TILES, members, OBS), bf16),
            pltpu.VMEM((BLOCKS // 2, 6 * OBS, 2 * CELLS), bf16),
            pltpu.VMEM((members, cells), bf16),
            pltpu.VMEM((members * BLOCKS, CELLS), f32),
            pltpu.VMEM((turn * BLOCKS, CELLS), f32),
            pltpu.VMEM((TILES * OBS, CELLS), f32),
            pltpu.VMEM((members * BLOCKS, CELLS), bf16),
            pltpu.VMEM((OBS // half, members), bf16),
            pltpu.VMEM((OBS // half, members), bf16),
            pltpu.VMEM((ROUNDS, turn // half, OBS), bf16),
            pltpu.VMEM((ROUNDS, turn // half, OBS), bf16),
            dma,
            dma,
            dma,
            dma,
            dma((8 + max(half, 2),)),
            dma((TILES,)),
            dma((ROUNDS, 8 + max(half, 2))),
            dma((ROUNDS, TILES)),
            dma((2,)),
            dma((ROUNDS, 2)),
        ],
        compiler_params=pltpu.CompilerParams(
            collective_id=0, has_side_effects=True, vmem_limit_bytes=44 << 20
        ),
    )(
        taper_radius,
        predicted[0, 0],
        observation_jitter[0, 0],
        measured_value[0],
        measurement_variance[0],
        obs_block,
        taper_pattern.reshape(BLOCKS, PATTERN),
        params.reshape(members * BLOCKS, CELLS),
    )
    out = regrouped.reshape(cols, share, BLK_X, BLK_Y, CELLS).transpose(1, 2, 0, 3, 4)
    return out.reshape(share, BLK_X, cols * BLK_Y, CELLS)


def solution(mesh):
    placed = (
        P(None, "gx", "gy", None),
        P("gx", "gy", None, None),
        P("gx", "gy", None),
        P("gx", "gy", None),
        P("gx", "gy", None, None),
        P(),
        P("gx", "gy"),
        P("gx", "gy", None),
    )
    body = functools.partial(per_device, mesh.shape["gx"], mesh.shape["gy"])
    return jax.shard_map(
        body, mesh=mesh, in_specs=placed, out_specs=P("gy", "gx", None, None), check_vma=False
    )
```

time: 180 us -> 126 us (0.70)
  the two profiles are of different devices: /device:TPU:57 before, /device:TPU:255 now
where the time goes in v2:
time: 126 us
  Pallas kernels  117 us (93%)
  local copies, waits for them, and re-layouts  9.05 us (7%)
    pallas_call x1, Pallas kernels, per_device(): pl.pallas_call(functools.partial(kernel, rows, cols), out_shape=jax.Shape...  117 us
    unnamed x16, local copies, waits for them, and re-layouts  7.07 us

profile of v2, /device:TPU:255, one launch (start us, length us, event | category | flops | bytes accessed | tf_op | source)
XLA Modules:
  0.0 125.8 jit_solution(10755604259872253694)
XLA Ops:
  0.0 0.0 copy-start
  0.0 1.4 %copy-done = bf16[768,2,4,128]{3,2,1,0:T(4,128)(2,1)S(1)} copy-done((bf16[768,2,4,128]{3,2,1,0:T(4,128)(2,1)S(1)}, bf16[768,2,4,128]{3,2,1,0:T(4,128)(2,1)}, u32[]{:S(2)}) %copy-start) | copy-done | bytes 1572888
  1.4 0.0 copy-start.1
  1.4 1.0 copy-done.1
  2.4 0.0 copy-start.2
  2.4 1.0 copy-done.2
  3.4 0.0 copy-start.3
  3.4 1.0 copy-done.3
  4.4 0.0 copy-start.4
  4.4 0.7 copy-done.4
  5.1 0.0 copy-start.5
  5.1 0.7 copy-done.5
  5.8 0.0 copy-start.6
  5.8 0.7 copy-done.6
  6.4 0.0 copy-start.7
  6.4 0.7 copy-done.7
  7.1 116.7 %shard_map.82 = bf16[48,128,128]{2,1,0:T(8,128)(2,1)S(1)} custom-call(s32[2,4]{1,0:T(2,128)S(1)} %copy-done.5, f32[768,128]{1,0:T(8,128)S(1)} %bitcast.12, f32[768,128]{1,0:T(8,128)S(1)} %bitcast.13, f32[1,128]{1,0:T(1,128)S(1)} %bitcast.15, f32[1,128]{1,0:T(1,128)S(1)} %bitcast.16, s32[16,48,128]{2,1,0:T(8,128)S(1)} %copy-done.3, s32[8,25]{1,0:T(8,128)S(1)} %bitcast.14, ...), custom_call_target="tpu_custom_call" | custom-call | tf_op jit(solution)/shard_map/pallas_call | solution.py:521
  123.8 2.0 %copy.9 = bf16[16,2,48,4,128]{4,3,2,1,0:T(4,128)(2,1)} copy(bf16[16,2,48,4,128]{4,3,1,0,2:T(4,128)(2,1)S(1)} %bitcast.10) | data formatting | bytes 3145728 | tf_op jit(solution)/shard_map/transpose | solution.py:564
Async XLA Ops:
  0.0 1.4 %copy-start = (bf16[768,2,4,128]{3,2,1,0:T(4,128)(2,1)S(1)}, bf16[768,2,4,128]{3,2,1,0:T(4,128)(2,1)}, u32[]{:S(2)}) copy-start(bf16[768,2,4,128]{3,2,1,0:T(4,128)(2,1)} %param.8) | copy-start | bytes 4718596
  1.4 1.0 copy-start.1
  2.4 1.0 copy-start.2
  3.4 1.0 copy-start.3
  4.4 0.7 copy-start.4
  5.1 0.7 copy-start.5
  5.8 0.7 copy-start.6
  6.4 0.7 copy-start.7

commit v3 on v2

--- a/solution.py
+++ b/solution.py
@@ -51,6 +51,15 @@
 def kernel(
     rows,
     cols,
+    radius_hbm,
+    pred_hbm,
+    jitter_hbm,
+    value_hbm,
+    var_hbm,
+    map_hbm,
+    pattern_hbm,
+    params_hbm,
+    recv_ref,
     radius_ref,
     pred_ref,
     jitter_ref,
@@ -58,8 +67,6 @@
     var_ref,
     map_ref,
     pattern_ref,
-    params_hbm,
-    recv_ref,
     params_ref,
     d_ref,
     w_ref,
@@ -71,8 +78,10 @@
     sent_ref,
     d_near,
     d_far,
-    w_near,
-    w_far,
+    w_near_first,
+    w_far_first,
+    w_near_rest,
+    w_far_rest,
     load_sem,
     own_sem,
     all_send,
@@ -81,8 +90,8 @@
     d_recv,
     w_send,
     w_recv,
-    d_relay,
-    w_relay,
+    d_cross,
+    w_cross,
 ):
     members = pred_ref.shape[0]
     piece = members // PIECES
@@ -96,6 +105,8 @@
     high_seam = gx == half
     seam = (gx == half - 1) | (gx == half)
     relay = jnp.logical_not(seam)
+    not_low_seam = jnp.logical_not(low_seam)
+    not_high_seam = jnp.logical_not(high_seam)
     column = lax.rem(gx, half)
     across = lax.rem(gx + half, rows)
     has_left = gy > 0
@@ -103,8 +114,23 @@
     sends_up = (gx > 0) & jnp.logical_not(high_seam)
     sends_down = (gx < rows - 1) & jnp.logical_not(low_seam)
 
-    params_load = pltpu.make_async_copy(params_hbm, params_ref, load_sem)
-    params_load.start()
+    loads = [
+        pltpu.make_async_copy(src, dst, load_sem.at[index])
+        for index, (src, dst) in enumerate(
+            (
+                (pred_hbm, pred_ref),
+                (var_hbm, var_ref),
+                (map_hbm, map_ref),
+                (jitter_hbm, jitter_ref),
+                (value_hbm, value_ref),
+                (radius_hbm, radius_ref),
+                (pattern_hbm, pattern_ref),
+                (params_hbm, params_ref),
+            )
+        )
+    ]
+    for load in loads:
+        load.start()
 
     barrier = pltpu.get_barrier_semaphore()
 
@@ -159,18 +185,26 @@
             device_id_type=MESH,
         )
 
+    def start(hops):
+        for there, hop in hops:
+
+            @pl.when(there)
+            def _(hop=hop):
+                hop.start()
+
+    def wait_sent(hops):
+        for there, hop in hops:
+
+            @pl.when(there)
+            def _(hop=hop):
+                hop.wait_send()
+
     class Parcel:
-        def __init__(self, buf, start, size, near, far, send, recv, relays):
-            self.buf, self.start, self.size = buf, start, size
-            self.near, self.far, self.send, self.recv, self.relays = near, far, send, recv, relays
-            self.part = size // half
+        def __init__(self, buf, begin, size, send, recv):
+            self.buf, self.begin, self.size, self.send, self.recv = buf, begin, size, send, recv
 
         def rows_of(self, slot):
-            return self.buf.at[slot, pl.ds(self.start, self.size), :]
-
-        def part_of(self, slot, index):
-            offset = pl.multiple_of(self.start + index * self.part, self.part)
-            return self.buf.at[slot, pl.ds(offset, self.part), :]
+            return self.buf.at[slot, pl.ds(self.begin, self.size), :]
 
         def hop(self, index, src, dst, dev):
             return remote(
@@ -185,102 +219,113 @@
                 (has_left, self.hop(3, CENTRE, 7, (gx, gy - 1))),
             )
 
-        def passed_hops(self):
+        def up_hops(self):
             return (
                 (has_right, self.hop(4, UP, 0, (gx, gy + 1))),
                 (has_left, self.hop(5, UP, 6, (gx, gy - 1))),
+            )
+
+        def down_hops(self):
+            return (
                 (has_right, self.hop(6, DOWN, 2, (gx, gy + 1))),
                 (has_left, self.hop(7, DOWN, 8, (gx, gy - 1))),
             )
 
-        def seam_hops(self):
+        def wait_slot(self, slot, there):
+            @pl.when(there)
+            def _():
+                ref = self.rows_of(slot)
+                pltpu.make_async_copy(ref, ref, self.recv.at[slot]).wait()
+
+        def pass_on(self):
+            self.wait_slot(UP, sends_up)
+            self.wait_slot(DOWN, sends_down)
+            start([(there & not_high_seam, hop) for there, hop in self.up_hops()])
+            start([(there & not_low_seam, hop) for there, hop in self.down_hops()])
+
+        def pass_on_seam(self):
+            start([(there & high_seam, hop) for there, hop in self.up_hops()])
+            start([(there & low_seam, hop) for there, hop in self.down_hops()])
+
+        def wait_sides(self):
+            for slot in (1, 0, 2):
+                self.wait_slot(slot, has_left)
+            for slot in (7, 6, 8):
+                self.wait_slot(slot, has_right)
+
+        def finish(self):
+            wait_sent(self.own_hops())
+            wait_sent(self.up_hops())
+            wait_sent(self.down_hops())
+
+    class Seam:
+        def __init__(self, buf, begin, size, near, far, send, sems):
+            self.buf, self.begin, self.size = buf, begin, size
+            self.near, self.far, self.send = near, far, send
+            self.near_sem, self.far_sem, self.slot_sem = sems.at[0], sems.at[1], sems.at[2]
+            self.part = size // half
+
+        def part_of(self, slot, index):
+            offset = pl.multiple_of(self.begin + index * self.part, self.part)
+            return self.buf.at[slot, pl.ds(offset, self.part), :]
+
+        def out_hops(self):
             hops = []
             for side, is_seam, at in ((0, low_seam, half - 1), (half, high_seam, half)):
                 for index in range(half):
                     if side + index == at:
-                        dst, recv, dev = self.far, self.relays.at[1], (across, gy)
+                        dst, recv, dev = self.far, self.far_sem, (across, gy)
                     else:
-                        dst, recv, dev = self.near, self.relays.at[0], (side + index, gy)
+                        dst, recv, dev = self.near, self.near_sem, (side + index, gy)
                     src = self.part_of(CENTRE, index)
-                    hops.append((is_seam, remote(src, dst, self.send.at[8 + index], recv, dev)))
+                    hops.append((is_seam, remote(src, dst, self.send.at[index], recv, dev)))
             return hops
 
         def cross_hops(self):
             low_end, high_end = gx == 0, gx == rows - 1
             inner = relay & jnp.logical_not(low_end) & jnp.logical_not(high_end)
-            send, dev = self.send.at[8], (across, gy)
+            send, dev = self.send.at[0], (across, gy)
+            to_up, to_down = self.part_of(UP, 0), self.part_of(DOWN, half - 1)
             return (
-                (inner, remote(self.near, self.far, send, self.relays.at[1], dev)),
-                (low_end, remote(self.near, self.part_of(UP, 0), send, self.recv.at[UP], dev)),
-                (
-                    high_end,
-                    remote(self.near, self.part_of(DOWN, half - 1), send, self.recv.at[DOWN], dev),
-                ),
+                (inner, remote(self.near, self.far, send, self.far_sem, dev)),
+                (low_end, remote(self.near, to_up, send, self.slot_sem, dev)),
+                (high_end, remote(self.near, to_down, send, self.slot_sem, dev)),
             )
 
         def last_hops(self):
             hops = []
             for is_side, at, slot in ((lower, half - 1, DOWN), (upper, half, UP)):
                 dst = self.part_of(slot, column)
-                hop = remote(self.far, dst, self.send.at[9], self.recv.at[slot], (at, gy))
+                hop = remote(self.far, dst, self.send.at[1], self.slot_sem, (at, gy))
                 hops.append((is_side & relay, hop))
             return hops
 
-        def wait_near(self):
+        def cross(self):
             @pl.when(relay)
             def _():
-                pltpu.make_async_copy(self.near, self.near, self.relays.at[0]).wait()
-
-        def wait_far(self):
+                pltpu.make_async_copy(self.near, self.near, self.near_sem).wait()
+
+            start(self.cross_hops())
+
+        def last(self):
             @pl.when(relay)
             def _():
-                pltpu.make_async_copy(self.far, self.far, self.relays.at[1]).wait()
-
-        def wait_slots(self, slots, where=None):
-            for slot in slots:
-                there = arrives[slot] if where is None else arrives[slot] & where
-
-                @pl.when(there)
+                pltpu.make_async_copy(self.far, self.far, self.far_sem).wait()
+
+            start(self.last_hops())
+
+        def wait_slot(self):
+            for is_seam, slot in ((high_seam, UP), (low_seam, DOWN)):
+
+                @pl.when(is_seam)
                 def _(slot=slot):
-                    ref = self.rows_of(slot)
-                    pltpu.make_async_copy(ref, ref, self.recv.at[slot]).wait()
-
-        def start_own(self):
-            start(self.own_hops())
-            start(self.seam_hops())
-
-        def cross(self):
-            self.wait_near()
-            start(self.cross_hops())
-
-        def last(self):
-            self.wait_far()
-            start(self.last_hops())
-
-        def pass_on(self, where):
-            self.wait_slots((UP, DOWN), where)
-            start(self.passed_hops(), where)
-
-        def wait_sent(self):
-            for hops in (
-                self.own_hops(),
-                self.passed_hops(),
-                self.seam_hops(),
-                self.cross_hops(),
-                self.last_hops(),
-            ):
-                for there, hop in hops:
-
-                    @pl.when(there)
-                    def _(hop=hop):
-                        hop.wait_send()
-
-    def start(hops, where=None):
-        for there, hop in hops:
-
-            @pl.when(there if where is None else there & where)
-            def _(hop=hop):
-                hop.start()
+                    ref = self.buf.at[slot, pl.ds(self.begin, self.size), :]
+                    pltpu.make_async_copy(ref, ref, self.slot_sem).wait()
+
+        def finish(self):
+            wait_sent(self.out_hops())
+            wait_sent(self.cross_hops())
+            wait_sent(self.last_hops())
 
     arrives = {UP: gx > 0, DOWN: gx < rows - 1}
     arrives.update({slot: has_left for slot in (0, 1, 2)})
@@ -293,28 +338,37 @@
             d_ref[slot] = jnp.zeros(d_ref.shape[1:], d_ref.dtype)
             w_ref[slot] = jnp.zeros(w_ref.shape[1:], w_ref.dtype)
 
-    d_parcel = Parcel(d_ref, 0, OBS, d_near, d_far, d_send, d_recv, d_relay)
+    turn_size = 2 * piece
+    d_parcel = Parcel(d_ref, 0, OBS, d_send, d_recv)
     w_parcels = [
-        Parcel(
-            w_ref,
-            turn * 2 * piece,
-            2 * piece,
-            w_near.at[turn],
-            w_far.at[turn],
-            w_send.at[turn],
-            w_recv.at[turn],
-            w_relay.at[turn],
-        )
+        Parcel(w_ref, turn * turn_size, turn_size, w_send.at[turn], w_recv.at[turn])
         for turn in range(ROUNDS)
     ]
-
+    d_seam = Seam(d_ref, 0, OBS, d_near, d_far, d_cross.at[0], d_cross.at[1])
+    w_first = Seam(
+        w_ref, 0, turn_size, w_near_first, w_far_first, w_cross.at[0], w_cross.at[1]
+    )
+    w_rest = Seam(
+        w_ref,
+        turn_size,
+        members - turn_size,
+        w_near_rest,
+        w_far_rest,
+        w_cross.at[2],
+        w_cross.at[3],
+    )
+
+    loads[0].wait()
     pred = pred_ref[...]
     deviation = pred - jnp.sum(pred, axis=0, keepdims=True) / members
     d_own = deviation.astype(jnp.bfloat16)
     d_turned = deviation.T.astype(jnp.bfloat16)
     d_ref[CENTRE] = d_turned
     pl.semaphore_wait(barrier, greetings)
-    d_parcel.start_own()
+    start(d_seam.out_hops())
+    start(d_parcel.own_hops())
+    for load in loads[1:]:
+        load.wait()
 
     gram = mm(d_turned, d_own) / (members - 1)
     own_map = jnp.broadcast_to(map_ref[gx, pl.ds(gy, 1), :].astype(jnp.float32), (OBS, OBS))
@@ -325,9 +379,9 @@
     variance = var_ref[...]
     system = jnp.where(own_map == own_map.T, gram, 0.0) + jnp.where(eye, variance, 0.0)
     inv, spread = newton_start(system, jnp.min(variance, axis=1, keepdims=True))
-    inv, spread = newton(system, inv, spread, 4)
-    d_parcel.cross()
-    inv, spread = newton(system, inv, spread, NEWTON - 4)
+    inv, spread = newton(system, inv, spread, 6)
+    d_seam.cross()
+    inv, spread = newton(system, inv, spread, NEWTON - 6)
     deviation_scale = jnp.sqrt(variance)
     for turn in range(ROUNDS):
         for place, which in enumerate((turn, PIECES - 1 - turn)):
@@ -337,10 +391,13 @@
             )
             at = (2 * turn + place) * piece
             w_ref[CENTRE, at : at + piece, :] = mm(residual, inv, EXACT).astype(jnp.bfloat16)
-        w_parcels[turn].start_own()
-
-    d_parcel.pass_on(relay)
-    d_parcel.last()
+        if turn == 0:
+            start(w_first.out_hops())
+        if turn == ROUNDS - 1:
+            start(w_rest.out_hops())
+        start(w_parcels[turn].own_hops())
+
+    d_parcel.pass_on()
 
     block = lax.broadcasted_iota(jnp.int32, (BLOCKS, OBS), 0)
     reach = jnp.zeros((BLOCKS, OBS), jnp.int32)
@@ -368,7 +425,6 @@
         filled = jnp.concatenate([taper, jnp.zeros((OBS - BLOCKS, OBS), jnp.float32)], axis=0)
         taper_ref[tile * OBS : (tile + 1) * OBS, :] = filled.T
 
-    params_load.wait()
     batch = 64
 
     def batch_rows(step):
@@ -414,18 +470,20 @@
                 cross[:, side * CELLS : (side + 1) * CELLS] * weight[:, index : index + 1]
             ).astype(jnp.bfloat16)
 
-    w_parcels[0].cross()
-    w_parcels[0].pass_on(relay)
-    w_parcels[1].cross()
-    d_parcel.pass_on(seam)
-    d_parcel.wait_slots((1, 7, 0, 2, 6, 8))
-    gain_of(0)
-    gain_of(1)
-    w_parcels[0].last()
-    w_parcels[1].pass_on(relay)
-    w_parcels[2].cross()
-    gain_of(2)
-    gain_of(3)
+    d_seam.last()
+    w_first.cross()
+    w_parcels[0].pass_on()
+    w_rest.cross()
+    w_first.last()
+    d_seam.wait_slot()
+    d_parcel.pass_on_seam()
+    w_parcels[1].pass_on()
+    w_parcels[2].pass_on()
+    w_first.wait_slot()
+    w_parcels[0].pass_on_seam()
+    d_parcel.wait_sides()
+    for group in range(BLOCKS // 2):
+        gain_of(group)
 
     fan = cols // PIECES
 
@@ -437,9 +495,8 @@
     far_side = lax.div(2 * gy, cols)
 
     def finish(turn):
-        w_parcels[turn].pass_on(seam)
-        w_parcels[turn].wait_slots((1, 7, 0, 2, 6, 8))
-        who = slice(turn * 2 * piece, (turn + 1) * 2 * piece)
+        w_parcels[turn].wait_sides()
+        who = slice(turn * turn_size, (turn + 1) * turn_size)
         for group in range(BLOCKS // 2):
             first = first_slot(group)
             w_set = jnp.concatenate(
@@ -481,16 +538,16 @@
             lax.fori_loop(0, fan, send, 0)
 
     finish(0)
-    w_parcels[1].last()
-    w_parcels[2].pass_on(relay)
+    w_rest.last()
+    w_rest.wait_slot()
+    w_parcels[1].pass_on_seam()
+    w_parcels[2].pass_on_seam()
     finish(1)
-    w_parcels[2].last()
     finish(2)
 
     others = recv_ref.at[pl.ds(0, cols - 1)]
-    d_parcel.wait_sent()
-    for parcel in w_parcels:
-        parcel.wait_sent()
+    for parcel in (d_parcel, *w_parcels, d_seam, w_first, w_rest):
+        parcel.finish()
     own_copy.wait()
     pltpu.make_async_copy(others, others, all_send).wait()
     pltpu.make_async_copy(others, others, all_recv).wait()
@@ -513,17 +570,22 @@
     half = rows // 2
     cells = BLOCKS * CELLS
     turn = members // ROUNDS
-    vmem = pl.BlockSpec(memory_space=pltpu.VMEM)
-    smem = pl.BlockSpec(memory_space=pltpu.SMEM)
-    anywhere = pl.BlockSpec(memory_space=pl.ANY)
+    hbm = pl.BlockSpec(memory_space=pltpu.HBM)
     dma = pltpu.SemaphoreType.DMA
     bf16, f32 = jnp.bfloat16, jnp.float32
     regrouped = pl.pallas_call(
         functools.partial(kernel, rows, cols),
         out_shape=jax.ShapeDtypeStruct((cols, share * BLOCKS, CELLS), bf16),
-        in_specs=[smem] + [vmem] * 6 + [anywhere],
-        out_specs=anywhere,
+        in_specs=[hbm] * 8,
+        out_specs=pl.BlockSpec(memory_space=pl.ANY),
         scratch_shapes=[
+            pltpu.SMEM((BLK_X, BLK_Y), jnp.int32),
+            pltpu.VMEM((members, OBS), f32),
+            pltpu.VMEM((members, OBS), f32),
+            pltpu.VMEM((1, OBS), f32),
+            pltpu.VMEM((1, OBS), f32),
+            pltpu.VMEM((rows, cols, OBS), jnp.int32),
+            pltpu.VMEM((BLOCKS, PATTERN), jnp.int32),
             pltpu.VMEM((members * BLOCKS, CELLS), bf16),
             pltpu.VMEM((TILES, OBS, members), bf16),
             pltpu.VMEM((TILES, members, OBS), bf16),
@@ -535,21 +597,23 @@
             pltpu.VMEM((members * BLOCKS, CELLS), bf16),
             pltpu.VMEM((OBS // half, members), bf16),
             pltpu.VMEM((OBS // half, members), bf16),
-            pltpu.VMEM((ROUNDS, turn // half, OBS), bf16),
-            pltpu.VMEM((ROUNDS, turn // half, OBS), bf16),
+            pltpu.VMEM((turn // half, OBS), bf16),
+            pltpu.VMEM((turn // half, OBS), bf16),
+            pltpu.VMEM((2 * turn // half, OBS), bf16),
+            pltpu.VMEM((2 * turn // half, OBS), bf16),
+            dma((8,)),
             dma,
             dma,
             dma,
-            dma,
-            dma((8 + max(half, 2),)),
+            dma((8,)),
             dma((TILES,)),
-            dma((ROUNDS, 8 + max(half, 2))),
+            dma((ROUNDS, 8)),
             dma((ROUNDS, TILES)),
-            dma((2,)),
-            dma((ROUNDS, 2)),
+            dma((2, max(half, 3))),
+            dma((4, max(half, 3))),
         ],
         compiler_params=pltpu.CompilerParams(
-            collective_id=0, has_side_effects=True, vmem_limit_bytes=44 << 20
+            collective_id=0, has_side_effects=True, vmem_limit_bytes=56 << 20
         ),
     )(
         taper_radius,

time: 126 us -> 101 us (0.80)
  the two profiles are of different devices: /device:TPU:255 before, /device:TPU:191 now
where the time goes in v3:
time: 101 us
  Pallas kernels  97.3 us (96%)
  local copies, waits for them, and re-layouts  3.37 us (3%)
    pallas_call x1, Pallas kernels, per_device(): pl.pallas_call(functools.partial(kernel, rows, cols), out_shape=jax.Shape...  97.3 us
    transpose x1, local copies, waits for them, and re-layouts, per_device(): regrouped.reshape(cols, share, BLK_X, BLK_Y, CELLS).transpose(1, 2, 0, 3, 4)  3.37 us

profile of v3, /device:TPU:191, one launch (start us, length us, event | category | flops | bytes accessed | tf_op | source)
XLA Modules:
  0.0 100.6 jit_solution(7076811540054567491)
XLA Ops:
  0.0 97.3 %shard_map.82 = bf16[48,128,128]{2,1,0:T(8,128)(2,1)} custom-call(s32[2,4]{1,0:T(2,128)} %radius_hbm.1, f32[768,128]{1,0:T(8,128)} %bitcast.12, f32[768,128]{1,0:T(8,128)} %bitcast.13, f32[1,128]{1,0:T(1,128)} %bitcast.15, f32[1,128]{1,0:T(1,128)} %bitcast.16, s32[16,48,128]{2,1,0:T(8,128)} %map_hbm.1, s32[8,25]{1,0:T(8,128)} %bitcast.14, ...), custom_call_target="tpu_custom_call" | custom-call | tf_op jit(solution)/shard_map/pallas_call | solution.py:576
  97.3 3.4 %copy.9 = bf16[16,2,48,4,128]{4,3,2,1,0:T(4,128)(2,1)} copy(bf16[16,2,48,4,128]{4,3,1,0,2:T(4,128)(2,1)} %bitcast.10) | data formatting | bytes 3145728 | tf_op jit(solution)/shard_map/transpose | solution.py:628

commit v4 on v3

--- a/solution.py
+++ b/solution.py
@@ -364,9 +364,6 @@
     d_own = deviation.astype(jnp.bfloat16)
     d_turned = deviation.T.astype(jnp.bfloat16)
     d_ref[CENTRE] = d_turned
-    pl.semaphore_wait(barrier, greetings)
-    start(d_seam.out_hops())
-    start(d_parcel.own_hops())
     for load in loads[1:]:
         load.wait()
 
@@ -379,9 +376,7 @@
     variance = var_ref[...]
     system = jnp.where(own_map == own_map.T, gram, 0.0) + jnp.where(eye, variance, 0.0)
     inv, spread = newton_start(system, jnp.min(variance, axis=1, keepdims=True))
-    inv, spread = newton(system, inv, spread, 6)
-    d_seam.cross()
-    inv, spread = newton(system, inv, spread, NEWTON - 6)
+    inv, _ = newton(system, inv, spread, NEWTON)
     deviation_scale = jnp.sqrt(variance)
     for turn in range(ROUNDS):
         for place, which in enumerate((turn, PIECES - 1 - turn)):
@@ -391,13 +386,15 @@
             )
             at = (2 * turn + place) * piece
             w_ref[CENTRE, at : at + piece, :] = mm(residual, inv, EXACT).astype(jnp.bfloat16)
-        if turn == 0:
-            start(w_first.out_hops())
-        if turn == ROUNDS - 1:
-            start(w_rest.out_hops())
-        start(w_parcels[turn].own_hops())
-
-    d_parcel.pass_on()
+
+    pl.semaphore_wait(barrier, greetings)
+    start(d_seam.out_hops())
+    start(w_first.out_hops())
+    start(d_parcel.own_hops())
+    start(w_parcels[0].own_hops())
+    start(w_rest.out_hops())
+    start(w_parcels[1].own_hops())
+    start(w_parcels[2].own_hops())
 
     block = lax.broadcasted_iota(jnp.int32, (BLOCKS, OBS), 0)
     reach = jnp.zeros((BLOCKS, OBS), jnp.int32)
@@ -470,10 +467,12 @@
                 cross[:, side * CELLS : (side + 1) * CELLS] * weight[:, index : index + 1]
             ).astype(jnp.bfloat16)
 
+    d_seam.cross()
+    w_first.cross()
+    d_parcel.pass_on()
+    w_rest.cross()
+    w_parcels[0].pass_on()
     d_seam.last()
-    w_first.cross()
-    w_parcels[0].pass_on()
-    w_rest.cross()
     w_first.last()
     d_seam.wait_slot()
     d_parcel.pass_on_seam()

time: 101 us -> 96.2 us (0.952)
  Pallas kernels: 97.3 us -> 92.6 us
    pallas_call x1, Pallas kernels: 97.3 us -> 92.6 us  [per_device(): pl.pallas_call(functools.partial(kernel, rows, cols), out_shape=jax.Shape...]
where the time goes in v4:
time: 96.2 us; the launch traced here: 96 us
  Pallas kernels  92.6 us (96%)
  local copies, waits for them, and re-layouts  3.37 us (4%)
    pallas_call x1, Pallas kernels, per_device(): pl.pallas_call(functools.partial(kernel, rows, cols), out_shape=jax.Shape...  92.6 us
    transpose x1, local copies, waits for them, and re-layouts, per_device(): regrouped.reshape(cols, share, BLK_X, BLK_Y, CELLS).transpose(1, 2, 0, 3, 4)  3.37 us

profile of v4, /device:TPU:191, one launch (start us, length us, event | category | flops | bytes accessed | tf_op | source)
XLA Modules:
  0.0 96.0 jit_solution(15438270406794132896)
XLA Ops:
  0.0 92.6 %shard_map.82 = bf16[48,128,128]{2,1,0:T(8,128)(2,1)} custom-call(s32[2,4]{1,0:T(2,128)} %radius_hbm.1, f32[768,128]{1,0:T(8,128)} %bitcast.12, f32[768,128]{1,0:T(8,128)} %bitcast.13, f32[1,128]{1,0:T(1,128)} %bitcast.15, f32[1,128]{1,0:T(1,128)} %bitcast.16, s32[16,48,128]{2,1,0:T(8,128)} %map_hbm.1, s32[8,25]{1,0:T(8,128)} %bitcast.14, ...), custom_call_target="tpu_custom_call" | custom-call | tf_op jit(solution)/shard_map/pallas_call | solution.py:575
  92.7 3.4 %copy.9 = bf16[16,2,48,4,128]{4,3,2,1,0:T(4,128)(2,1)} copy(bf16[16,2,48,4,128]{4,3,1,0,2:T(4,128)(2,1)} %bitcast.10) | data formatting | bytes 3145728 | tf_op jit(solution)/shard_map/transpose | solution.py:627
